TPU v7x, 512 devices: a whole 4x4x16 slice. The times are simulated.
512 devices in a mesh: band: 16 (over z_hi, x, core), dom: 32 (over z_lo, y).
Axes of the slice: x: 4, y: 4, z: 16 (z_hi: 2, z_lo: 8; z = z_hi * 8 + z_lo), core: 2. Of those that a mesh axis runs over, the one named last changes fastest.
Arguments:
- orbitals: bfloat16 [20, 32, 8, 8, 4096], P(None, 'dom', None, None, 'band'), may hold values from -6 to 6
- rotation: bfloat16 [4096, 4096], P(None, 'band'), may hold values from -0.09375 to 0.09375
- potential: float32 [8, 32, 8, 8], P(None, 'dom'), may hold values from -4 to 4
Outputs:
- filtered: float32 [8, 32, 8, 8, 4096], P(None, 'dom', None, None, 'band')
All inputs are finite; a program needn't handle non-finite values.
Results may differ from a plain program's by a relative error of at most 0.0003.
Values may be sent and summed in bfloat16 or wider, within the bound.
No kernel may reach another device: no remote copies, remote signals or barrier semaphores. Data moves between devices by JAX's collectives and lax.ppermute only.
A program may use at most 64 MiB of HBM per device.

v0:
```python
import jax
import jax.numpy as jnp
from jax import lax
from jax.sharding import PartitionSpec as P

TILES_Y = 4


stencil_weights = (
    -5369.0 / 1800.0,
    12.0 / 7.0,
    -15.0 / 56.0,
    10.0 / 189.0,
    -1.0 / 112.0,
    2.0 / 1925.0,
    -1.0 / 16632.0,
)
inverse_spacing = 4.0
centre_shift = 20.0
spread_scale = 24.0


def from_behind(value, axis, steps):
    count = lax.axis_size(axis)
    initial, last = (max(0, -steps), min(count, count - steps))
    return lax.ppermute(value, axis, [(source, source + steps) for source in range(initial, last)])


def apply_filter(slab_local, potential_local, fetch):
    reach = len(stencil_weights) - 1
    planes = potential_local.shape[0]
    extent_first = slab_local.shape[1]
    extent_second = slab_local.shape[2]
    middle = slab_local[reach : reach + planes]
    tile_row = lax.axis_index("dom") % TILES_Y
    below_first = fetch(middle[:, extent_first - reach :], TILES_Y)
    above_first = fetch(middle[:, :reach], -TILES_Y)
    below_second = fetch(middle[:, :, extent_second - reach :], 1)
    above_second = fetch(middle[:, :, :reach], -1)
    below_second = jnp.where(tile_row == 0, jnp.zeros_like(below_second), below_second)
    above_second = jnp.where(tile_row == TILES_Y - 1, jnp.zeros_like(above_second), above_second)
    widened_first = jnp.concatenate([below_first, middle, above_first], axis=1)
    widened_second = jnp.concatenate([below_second, middle, above_second], axis=2)
    accumulated = 3.0 * stencil_weights[0] * middle
    for offset in range(1, reach + 1):
        neighbours = slab_local[reach + offset : reach + offset + planes]
        neighbours = neighbours + slab_local[reach - offset : reach - offset + planes]
        neighbours = neighbours + widened_first[:, reach + offset : reach + offset + extent_first]
        neighbours = neighbours + widened_first[:, reach - offset : reach - offset + extent_first]
        neighbours = (
            neighbours + widened_second[:, :, reach + offset : reach + offset + extent_second]
        )
        neighbours = (
            neighbours + widened_second[:, :, reach - offset : reach - offset + extent_second]
        )
        accumulated = accumulated + stencil_weights[offset] * neighbours
    hamiltonian = (
        -0.5 * inverse_spacing * accumulated + (potential_local[..., None] - centre_shift) * middle
    )
    return hamiltonian / spread_scale


def on_device(orbitals, rotation, potential):
    ghosted = orbitals.shape[0]
    extent_first = orbitals.shape[2]
    extent_second = orbitals.shape[3]
    columns = orbitals.shape[4]
    planes = potential.shape[0]
    new_columns = rotation.shape[1]
    slab_local = orbitals.reshape(ghosted, extent_first, extent_second, columns)
    potential_local = potential.reshape(planes, extent_first, extent_second)
    flattened = slab_local.reshape(ghosted * extent_first * extent_second, columns)
    rotated = jnp.dot(
        lax.all_gather(flattened, "band", axis=1, tiled=True),
        rotation,
        preferred_element_type=jnp.float32,
    )
    rotated = rotated.reshape(ghosted, extent_first, extent_second, new_columns)

    def fetch_rotated(portion, distance):
        return from_behind(portion, "dom", distance)

    result = apply_filter(rotated, potential_local, fetch_rotated)
    return result.reshape(planes, 1, extent_first, extent_second, new_columns)


def solution(mesh):
    in_specs = (P(None, "dom", None, None, "band"), P(None, "band"), P(None, "dom", None, None))
    out_specs = P(None, "dom", None, None, "band")
    return jax.shard_map(
        on_device, mesh=mesh, in_specs=in_specs, out_specs=out_specs, check_vma=False
    )
```

profile of v0, /device:TPU:64, one launch (start us, length us, event | category | flops | bytes accessed | tf_op | source)
XLA Modules:
  0.0 275.1 jit_solution(16084971167236357317)
XLA Ops:
  6.5 0.0 copy-start
  6.5 0.0 all-gather.2.cloned.1.call-start
  6.5 0.7 all-gather.2.cloned.1.call-update
  7.3 217.0 %all-gather.2.cloned.1.call-done = bf16[1280,4096]{1,0:T(8,128)(2,1)} async-done(((bf16[1280,256]{1,0:T(8,128)(2,1)}), bf16[1280,4096]{1,0:T(8,128)(2,1)}) %all-gather.2.cloned.1.call-update) | async-done | bytes 10485776 | tf_op jit(solution)/shard_map/all_gather | solution.py:74
  224.3 0.0 copy-done
  224.3 5.6 %fusion.62 = f32[1280,256]{1,0:T(8,128)S(1)} fusion(bf16[1280,4096]{1,0:T(8,128)(2,1)} %all-gather.2.cloned.1.call-done, bf16[4096,256]{1,0:T(8,128)(2,1)S(1)} %copy-done), kind=kOutput, calls=%fused_computation.115 | convolution fusion | flops 2684354560 | bytes 13893632 | tf_op jit(solution)/shard_map/dot_general | solution.py:73
  229.9 0.4 slice_add_fusion
  230.3 0.0 copy-start.1
  230.3 0.1 fusion.60
  230.4 3.4 %collective-permute-start.3 = (f32[8,8,6,256]{3,2,1,0:T(8,128)S(1)}, f32[8,8,6,256]{3,2,1,0:T(8,128)S(1)}, u32[]{:S(2)}, u32[]{:S(2)}) collective-permute-start(f32[8,8,6,256]{3,2,1,0:T(8,128)S(1)} %get-tuple-element.13), channel_id=1, source_target_pairs={{0,1},{1,2},{2,3},{3,4},{4,5},{5,6},{6,7},{7,8},{8,9},{9,10},{10,1... | collective-permute-start | bytes 1179656 | tf_op jit(solution)/shard_map/ppermute | solution.py:26
  233.8 0.0 copy-done.1
  233.8 4.6 %collective-permute-start.2 = (f32[8,8,6,256]{3,2,1,0:T(8,128)S(1)}, f32[8,8,6,256]{3,2,1,0:T(8,128)S(1)}, u32[]{:S(2)}, u32[]{:S(2)}) collective-permute-start(f32[8,8,6,256]{3,2,1,0:T(8,128)S(1)} %get-tuple-element.12), channel_id=1, source_target_pairs={{1,0},{2,1},{3,2},{4,3},{5,4},{6,5},{7,6},{8,7},{9,8},{10,9},{11,1... | collective-permute-start | bytes 1179656 | tf_op jit(solution)/shard_map/ppermute | solution.py:26
  238.4 0.1 fusion.61
  238.4 9.1 %collective-permute-start.1 = (f32[8,6,8,256]{3,2,1,0:T(8,128)S(1)}, f32[8,6,8,256]{3,2,1,0:T(8,128)S(1)}, u32[]{:S(2)}, u32[]{:S(2)}) collective-permute-start(f32[8,6,8,256]{3,2,1,0:T(8,128)S(1)} %get-tuple-element.15), channel_id=1, source_target_pairs={{0,4},{1,5},{2,6},{3,7},{4,8},{5,9},{6,10},{7,11},{8,12},{9,13},{1... | collective-permute-start | bytes 1179656 | tf_op jit(solution)/shard_map/ppermute | solution.py:26
  247.5 1.9 collective-permute-start
  249.5 0.0 collective-permute-done.3
  249.5 0.1 broadcast_select_fusion
  249.5 0.6 collective-permute-done.2
  250.1 0.1 broadcast_select_fusion.1
  250.2 5.6 %collective-permute-done.1 = f32[8,6,8,256]{3,2,1,0:T(8,128)S(1)} collective-permute-done((f32[8,6,8,256]{3,2,1,0:T(8,128)S(1)}, f32[8,6,8,256]{3,2,1,0:T(8,128)S(1)}, u32[]{:S(2)}, u32[]{:S(2)}) %collective-permute-start.1) | collective-permute-done | bytes 393248 | tf_op jit(solution)/shard_map/ppermute | solution.py:26
  255.7 10.0 %collective-permute-done = f32[8,6,8,256]{3,2,1,0:T(8,128)S(1)} collective-permute-done((f32[8,6,8,256]{3,2,1,0:T(8,128)S(1)}, f32[8,6,8,256]{3,2,1,0:T(8,128)S(1)}, u32[]{:S(2)}, u32[]{:S(2)}) %collective-permute-start) | collective-permute-done | bytes 393248 | tf_op jit(solution)/shard_map/ppermute | solution.py:26
  265.7 2.5 fusion.10
  (1 shorter events, 0.0 us)
Async XLA Ops:
  6.5 217.8 %copy-start = (bf16[4096,256]{1,0:T(8,128)(2,1)S(1)}, bf16[4096,256]{1,0:T(8,128)(2,1)}, u32[]{:S(2)}) copy-start(bf16[4096,256]{1,0:T(8,128)(2,1)} %param.4) | copy-start | bytes 6291460
  6.5 217.8 %all-gather.2.cloned.1.call-start = ((), (), s32[]{:S(2)}) async-start(), calls=%async_computation | async-start | bytes 11141120 | tf_op jit(solution)/shard_map/all_gather | solution.py:74
  230.3 3.5 %copy-start.1 = (f32[8,1,8,8]{3,2,1,0:T(8,128)S(1)}, f32[8,1,8,8]{3,2,1,0:T(8,128)}, u32[]{:S(2)}) copy-start(f32[8,1,8,8]{3,2,1,0:T(8,128)} %param.5) | copy-start | bytes 6148
  230.4 19.1 %collective-permute-start.3 = (f32[8,8,6,256]{3,2,1,0:T(8,128)S(1)}, f32[8,8,6,256]{3,2,1,0:T(8,128)S(1)}, u32[]{:S(2)}, u32[]{:S(2)}) collective-permute-start(f32[8,8,6,256]{3,2,1,0:T(8,128)S(1)} %get-tuple-element.13), channel_id=1, source_target_pairs={{0,1},{1,2},{2,3},{3,4},{4,5},{5,6},{6,7},{7,8},{8,9},{9,10},{10,1... | collective-permute-start | bytes 1179656 | tf_op jit(solution)/shard_map/ppermute | solution.py:26
  233.8 16.3 %collective-permute-start.2 = (f32[8,8,6,256]{3,2,1,0:T(8,128)S(1)}, f32[8,8,6,256]{3,2,1,0:T(8,128)S(1)}, u32[]{:S(2)}, u32[]{:S(2)}) collective-permute-start(f32[8,8,6,256]{3,2,1,0:T(8,128)S(1)} %get-tuple-element.12), channel_id=1, source_target_pairs={{1,0},{2,1},{3,2},{4,3},{5,4},{6,5},{7,6},{8,7},{9,8},{10,9},{11,1... | collective-permute-start | bytes 1179656 | tf_op jit(solution)/shard_map/ppermute | solution.py:26
  238.4 17.3 %collective-permute-start.1 = (f32[8,6,8,256]{3,2,1,0:T(8,128)S(1)}, f32[8,6,8,256]{3,2,1,0:T(8,128)S(1)}, u32[]{:S(2)}, u32[]{:S(2)}) collective-permute-start(f32[8,6,8,256]{3,2,1,0:T(8,128)S(1)} %get-tuple-element.15), channel_id=1, source_target_pairs={{0,4},{1,5},{2,6},{3,7},{4,8},{5,9},{6,10},{7,11},{8,12},{9,13},{1... | collective-permute-start | bytes 1179656 | tf_op jit(solution)/shard_map/ppermute | solution.py:26
  247.5 18.2 %collective-permute-start = (f32[8,6,8,256]{3,2,1,0:T(8,128)S(1)}, f32[8,6,8,256]{3,2,1,0:T(8,128)S(1)}, u32[]{:S(2)}, u32[]{:S(2)}) collective-permute-start(f32[8,6,8,256]{3,2,1,0:T(8,128)S(1)} %get-tuple-element.14), channel_id=1, source_target_pairs={{4,0},{5,1},{6,2},{7,3},{8,4},{9,5},{10,6},{11,7},{12,8},{13,9},{1... | collective-permute-start | bytes 1179656 | tf_op jit(solution)/shard_map/ppermute | solution.py:26
Sparse Core Ops, SparseCore 0:
  10.5 213.7 all-gather.1
where the time goes:
time: 275 us
  waiting for transfers between devices  234 us (85%)
  starting transfers between devices  19 us (7%)
  between operations  13.5 us (5%)
  matrix products  5.59 us (2%)
  other arithmetic  2.97 us (1%)
    all_gather x1, waiting for transfers between devices, on_device(): lax.all_gather(flattened, 'band', axis=1, tiled=True)  217 us
    ppermute x4, starting transfers between devices, from_behind(): lax.ppermute(value, axis, [(source, source + steps) for source in range(i...  18.9 us
    ppermute x4, waiting for transfers between devices, from_behind(): lax.ppermute(value, axis, [(source, source + steps) for source in range(i...  16.1 us
    dot_general x1, matrix products, on_device(): jnp.dot(lax.all_gather(flattened, 'band', axis=1, tiled=True), rotation,...  5.59 us
  transfers between devices with their start and end apart: 5, of which 4 were waited for; matrix products, arithmetic and copies ran while one was open for 0% of the time, Pallas kernels for 0%

commit v1 on v0

v1 whole, which is shorter than its diff:
```python
import jax
import jax.numpy as jnp
from jax import lax
from jax.sharding import PartitionSpec as P

TILES_Y = 4


stencil_weights = (
    -5369.0 / 1800.0,
    12.0 / 7.0,
    -15.0 / 56.0,
    10.0 / 189.0,
    -1.0 / 112.0,
    2.0 / 1925.0,
    -1.0 / 16632.0,
)
inverse_spacing = 4.0
centre_shift = 20.0
spread_scale = 24.0

HALVES = 2
SIDE = 8
TAIL = 8

side_groups = [[h * SIDE + i for i in range(SIDE)] for h in range(HALVES)]
half_swap = [(b, (b + SIDE) % (HALVES * SIDE)) for b in range(HALVES * SIDE)]


def from_behind(value, axis, steps):
    count = lax.axis_size(axis)
    initial, last = (max(0, -steps), min(count, count - steps))
    return lax.ppermute(value, axis, [(source, source + steps) for source in range(initial, last)])


def along_y(value, steps):
    count = lax.axis_size("dom")
    pairs = [
        (source, source + steps)
        for source in range(count)
        if 0 <= source % TILES_Y + steps < TILES_Y
    ]
    return lax.ppermute(value, "dom", pairs)


def apply_filter(slab_local, potential_local):
    reach = len(stencil_weights) - 1
    planes = potential_local.shape[0]
    extent_first = slab_local.shape[1]
    extent_second = slab_local.shape[2]
    middle = slab_local[reach : reach + planes]
    below_first = from_behind(middle[:, extent_first - reach :], "dom", TILES_Y)
    above_first = from_behind(middle[:, :reach], "dom", -TILES_Y)
    below_second = along_y(middle[:, :, extent_second - reach :], 1)
    above_second = along_y(middle[:, :, :reach], -1)
    wide = jnp.float32
    widened_first = jnp.concatenate([below_first, middle, above_first], axis=1).astype(wide)
    widened_second = jnp.concatenate([below_second, middle, above_second], axis=2).astype(wide)
    slab = slab_local.astype(wide)
    centre = middle.astype(wide)
    accumulated = 3.0 * stencil_weights[0] * centre
    for offset in range(1, reach + 1):
        neighbours = slab[reach + offset : reach + offset + planes]
        neighbours = neighbours + slab[reach - offset : reach - offset + planes]
        neighbours = neighbours + widened_first[:, reach + offset : reach + offset + extent_first]
        neighbours = neighbours + widened_first[:, reach - offset : reach - offset + extent_first]
        neighbours = (
            neighbours + widened_second[:, :, reach + offset : reach + offset + extent_second]
        )
        neighbours = (
            neighbours + widened_second[:, :, reach - offset : reach - offset + extent_second]
        )
        accumulated = accumulated + stencil_weights[offset] * neighbours
    hamiltonian = (
        -0.5 * inverse_spacing * accumulated + (potential_local[..., None] - centre_shift) * centre
    )
    return hamiltonian / spread_scale


def encode(value):
    largest = jnp.max(jnp.abs(value))
    exponent = jnp.floor(jnp.log2(jnp.maximum(largest, 2.0**-100))) - 14.0
    scaled = (value * jnp.exp2(-exponent)).astype(jnp.float16)
    tail = jnp.broadcast_to(exponent.astype(jnp.float16), (TAIL, value.shape[1]))
    return jnp.concatenate([scaled, tail], axis=0)


def spread(code):
    return lax.all_gather(code, "band", axis=0, axis_index_groups=side_groups)


def product(codes, matrix, rows):
    exponent = codes[:, rows : rows + 1, :1].astype(jnp.float32)
    value = codes[:, :rows].astype(jnp.float32) * jnp.exp2(exponent)
    high = lax.reduce_precision(value, 8, 7)
    low = (value - high).astype(jnp.bfloat16)
    high = high.astype(jnp.bfloat16)
    dims = (((0, 2), (0, 1)), ((), ()))
    first = lax.dot_general(high, matrix, dims, preferred_element_type=jnp.float32)
    second = lax.dot_general(low, matrix, dims, preferred_element_type=jnp.float32)
    return first + second


def on_device(orbitals, rotation, potential):
    ghosted = orbitals.shape[0]
    extent_first = orbitals.shape[2]
    extent_second = orbitals.shape[3]
    columns = orbitals.shape[4]
    planes = potential.shape[0]
    new_columns = rotation.shape[1]
    rows = planes * extent_first * extent_second
    slab_local = orbitals.reshape(ghosted, extent_first, extent_second, columns)
    potential_local = potential.reshape(planes, extent_first, extent_second)

    filtered = apply_filter(slab_local, potential_local).reshape(rows, columns)
    code = encode(filtered)
    rotation, code = lax.optimization_barrier((rotation, code))
    half = lax.axis_index("band") // SIDE
    halves = rotation.reshape(HALVES, SIDE, columns, new_columns)
    arrived = lax.ppermute(code, "band", half_swap)
    gathered = spread(code)
    own_matrix = lax.dynamic_index_in_dim(halves, half, 0, keepdims=False)
    own = product(gathered, own_matrix, rows)
    gathered = spread(arrived)
    other_matrix = lax.dynamic_index_in_dim(halves, 1 - half, 0, keepdims=False)
    result = own + product(gathered, other_matrix, rows)
    return result.reshape(planes, 1, extent_first, extent_second, new_columns)


def solution(mesh):
    in_specs = (P(None, "dom", None, None, "band"), P(None, "band"), P(None, "dom", None, None))
    out_specs = P(None, "dom", None, None, "band")
    return jax.shard_map(
        on_device, mesh=mesh, in_specs=in_specs, out_specs=out_specs, check_vma=False
    )
```

time: 275 us -> 87.2 us (0.32)
  the two profiles are of different devices: /device:TPU:64 before, /device:TPU:33 now
where the time goes in v1:
time: 87.2 us; the launch traced here: 86.8 us
  blocking collectives  37.2 us (43%)
  starting transfers between devices  26.4 us (30%)
  other arithmetic  9.63 us (11%)
  waiting for transfers between devices  5.69 us (7%)
  matrix products  3.99 us (5%)
  local copies, waits for them, and re-layouts  2.9 us (3%)
  between operations  0.94 us (1%)
    all_gather x2, blocking collectives, spread(): return lax.all_gather(code, 'band', axis=0, axis_index_groups=side_groups)  37.2 us
    ppermute x1, starting transfers between devices, on_device(): arrived = lax.ppermute(code, 'band', half_swap)  15.2 us
    ppermute x2, starting transfers between devices, from_behind(): lax.ppermute(value, axis, [(source, source + steps) for source in range(i...  6.07 us
    ppermute x2, starting transfers between devices, along_y(): return lax.ppermute(value, 'dom', pairs)  5.18 us
    reduce_max x1, other arithmetic, encode(): largest = jnp.max(jnp.abs(value))  4.14 us
    ppermute x2, waiting for transfers between devices, along_y(): return lax.ppermute(value, 'dom', pairs)  3.87 us
    dot_general x2, matrix products, product(): lax.dot_general(high, matrix, dims, preferred_element_type=jnp.float32)  2.34 us
    ppermute x1, waiting for transfers between devices, on_device(): arrived = lax.ppermute(code, 'band', half_swap)  1.82 us
  transfers between devices with their start and end apart: 5, of which 2 were waited for; matrix products, arithmetic and copies ran while one was open for 6% of the time, Pallas kernels for 0%

profile of v1, /device:TPU:33, one launch (start us, length us, event | category | flops | bytes accessed | tf_op | source)
XLA Modules:
  0.0 86.8 jit_solution(9814512236120026912)
XLA Ops:
  0.0 0.0 copy-start
  0.0 1.1 %slice_bitcast_fusion = bf16[8,8,8,256]{3,2,1,0:T(8,128)(2,1)S(1)} fusion(bf16[20,1,8,8,256]{4,3,2,0,1:T(8,128)(2,1)} %bitcast.90), kind=kLoop, calls=%fused_computation.92 | loop fusion | bytes 524288 | tf_op jit(solution)/shard_map/slice | solution.py:51
  1.1 0.0 copy-start.1
  1.1 0.8 fusion.68
  2.0 3.5 %collective-permute-start = (bf16[8,6,8,256]{3,2,1,0:T(8,128)(2,1)}, bf16[8,6,8,256]{3,2,1,0:T(8,128)(2,1)}, u32[]{:S(2)}, u32[]{:S(2)}) collective-permute-start(bf16[8,6,8,256]{3,2,1,0:T(8,128)(2,1)} %get-tuple-element.13), channel_id=1, source_target_pairs={{0,4},{1,5},{2,6},{3,7},{4,8},{5,9},{6,10},{7,11},{8,12},{9,13},{1... | collective-permute-start | bytes 589832 | tf_op jit(solution)/shard_map/ppermute | solution.py:33
  5.5 0.0 copy-start.5
  5.5 2.5 %collective-permute-start.1 = (bf16[8,6,8,256]{3,2,1,0:T(8,128)(2,1)}, bf16[8,6,8,256]{3,2,1,0:T(8,128)(2,1)}, u32[]{:S(2)}, u32[]{:S(2)}) collective-permute-start(bf16[8,6,8,256]{3,2,1,0:T(8,128)(2,1)} %get-tuple-element.14), channel_id=1, source_target_pairs={{4,0},{5,1},{6,2},{7,3},{8,4},{9,5},{10,6},{11,7},{12,8},{13,9},{1... | collective-permute-start | bytes 589832 | tf_op jit(solution)/shard_map/ppermute | solution.py:33
  8.1 0.9 %fusion.69 = (bf16[8,8,6,256]{3,2,1,0:T(8,128)(2,1)}, bf16[8,8,6,256]{3,2,1,0:T(8,128)(2,1)}) fusion(bf16[8,8,8,256]{3,2,1,0:T(8,128)(2,1)S(1)} %slice_bitcast_fusion), kind=kLoop, calls=%fused_computation.107 | loop fusion | bytes 786432 | tf_op jit(solution)/shard_map/slice | solution.py:54
  8.9 3.9 %collective-permute-start.2 = (bf16[8,8,6,256]{3,2,1,0:T(8,128)(2,1)}, bf16[8,8,6,256]{3,2,1,0:T(8,128)(2,1)}, u32[]{:S(2)}, u32[]{:S(2)}) collective-permute-start(bf16[8,8,6,256]{3,2,1,0:T(8,128)(2,1)} %get-tuple-element.15), channel_id=1, source_target_pairs={{0,1},{1,2},{2,3},{4,5},{5,6},{6,7},{8,9},{9,10},{10,11},{12,13},{... | collective-permute-start | bytes 589832 | tf_op jit(solution)/shard_map/ppermute | solution.py:43
  12.8 0.0 copy-done.1
  12.8 1.3 %collective-permute-start.3 = (bf16[8,8,6,256]{3,2,1,0:T(8,128)(2,1)}, bf16[8,8,6,256]{3,2,1,0:T(8,128)(2,1)}, u32[]{:S(2)}, u32[]{:S(2)}) collective-permute-start(bf16[8,8,6,256]{3,2,1,0:T(8,128)(2,1)} %get-tuple-element.16), channel_id=1, source_target_pairs={{1,0},{2,1},{3,2},{5,4},{6,5},{7,6},{9,8},{10,9},{11,10},{13,12},{... | collective-permute-start | bytes 589832 | tf_op jit(solution)/shard_map/ppermute | solution.py:43
  14.1 0.0 copy-done.4
  14.1 1.4 %convert_bitcast_fusion = (f32[20,1,8,8,256]{4,3,2,0,1:T(8,128)S(1)}, f32[20,1,8,8,256]{4,3,2,1,0:T(8,128)}) fusion(bf16[20,1,8,8,256]{4,3,2,1,0:T(8,128)(2,1)S(1)} %copy-done.4), kind=kLoop, calls=%fused_computation.91 | loop fusion | flops 327680 | bytes 3276800 | tf_op jit(solution)/shard_map/convert_element_type | solution.py:59
  15.5 0.0 collective-permute-done
  15.6 0.0 collective-permute-done.1
  15.6 1.3 %maximum_convert_fusion.1 = f32[8,20,8,256]{3,2,1,0:T(8,128)S(1)} fusion(bf16[8,6,8,256]{3,2,1,0:T(8,128)(2,1)} %collective-permute-done.1, bf16[8,8,8,256]{3,2,1,0:T(8,128)(2,1)} %copy-done.1, bf16[8,6,8,256]{3,2,1,0:T(8,128)(2,1)} %collective-permute-done), kind=kLoop, calls=%fused_computation.38 | loop fusion | flops 983040 | bytes 1966080 | tf_op jit(solution)/shard_map/convert_element_type | solution.py:57
  16.9 0.0 collective-permute-done.2
  16.9 3.9 %collective-permute-done.3 = bf16[8,8,6,256]{3,2,1,0:T(8,128)(2,1)} collective-permute-done((bf16[8,8,6,256]{3,2,1,0:T(8,128)(2,1)}, bf16[8,8,6,256]{3,2,1,0:T(8,128)(2,1)}, u32[]{:S(2)}, u32[]{:S(2)}) %collective-permute-start.3) | collective-permute-done | bytes 196640 | tf_op jit(solution)/shard_map/ppermute | solution.py:43
  20.8 1.4 %maximum_convert_fusion = f32[8,8,20,256]{3,2,1,0:T(8,128)S(1)} fusion(bf16[8,8,6,256]{3,2,1,0:T(8,128)(2,1)} %collective-permute-done.3, bf16[8,8,8,256]{3,2,1,0:T(8,128)(2,1)S(1)} %copy-done.2, bf16[8,8,6,256]{3,2,1,0:T(8,128)(2,1)} %collective-permute-done.2), kind=kLoop, calls=%fused_computation.35 | loop fusion | flops 1966080 | bytes 1966080 | tf_op jit(solution)/shard_map/convert_element_type | solution.py:58
  22.2 4.1 %abs_reduce_fusion = (f32[]{:T(128)}, f32[8,8,8,256]{3,2,1,0:T(8,128)}) fusion(f32[8,8,8]{2,1,0:T(8,128)S(1)} %add_bitcast_fusion, f32[8,8,20,256]{3,2,1,0:T(8,128)S(1)} %maximum_convert_fusion, f32[8,20,8,256]{3,2,1,0:T(8,128)S(1)} %maximum_convert_fusion.1, f32[20,1,8,8,256]{4,3,2,1,0:T(8,128)S(1)} %copy-done.3, ...), kind=kLoop, calls=%fused_computation.90 | loop fusion | flops 6553599 | bytes 19662852 | tf_op jit(solution)/shard_map/reduce_max | solution.py:81
  27.1 1.1 %multiply_convert_fusion = f16[8,8,8,256]{3,2,1,0:T(8,128)(2,1)S(1)} fusion(f32[8,8,8,256]{3,2,1,0:T(8,128)} %get-tuple-element.10, f32[]{:T(128)S(6)} %mul.103), kind=kLoop, calls=%fused_computation.89 | loop fusion | flops 262144 | bytes 786436 | tf_op jit(solution)/shard_map/convert_element_type | solution.py:83
  28.2 0.1 concatenate.11
  28.3 15.2 %collective-permute-start.4 = (f16[520,256]{1,0:T(8,128)(2,1)S(1)}, f16[520,256]{1,0:T(8,128)(2,1)S(1)}, u32[]{:S(2)}, u32[]{:S(2)}) collective-permute-start(f16[520,256]{1,0:T(8,128)(2,1)S(1)} %concatenate.11), channel_id=1, source_target_pairs={{0,256},{32,288},{64,320},{96,352},{128,384},{160,416},{192,448},{... | collective-permute-start | bytes 798728 | tf_op jit(solution)/shard_map/ppermute | solution.py:120
  43.4 19.3 %all-gather.5 = f16[4160,256]{1,0:T(8,128)(2,1)S(1)} all-gather(f16[520,256]{1,0:T(8,128)(2,1)S(1)} %concatenate.11), channel_id=2, replica_groups={{0,32,64,96,128,160,192,224},{256,288,320,352,384,416,448,480},{1,33,65..., dimensions={0}, use_global_device_ids=true | all-gather | bytes 2396160 | tf_op jit(solution)/shard_map/all_gather | solution.py:89
  62.7 0.1 fusion.61
  62.8 0.8 fusion.17
  63.6 0.8 fusion.24
  64.5 1.8 %collective-permute-done.4 = f16[520,256]{1,0:T(8,128)(2,1)S(1)} collective-permute-done((f16[520,256]{1,0:T(8,128)(2,1)S(1)}, f16[520,256]{1,0:T(8,128)(2,1)S(1)}, u32[]{:S(2)}, u32[]{:S(2)}) %collective-permute-start.4) | collective-permute-done | bytes 266272 | tf_op jit(solution)/shard_map/ppermute | solution.py:120
  66.3 18.0 %all-gather.4 = f16[4160,256]{1,0:T(8,128)(2,1)S(1)} all-gather(f16[520,256]{1,0:T(8,128)(2,1)S(1)} %collective-permute-done.4), channel_id=3, replica_groups={{0,32,64,96,128,160,192,224},{256,288,320,352,384,416,448,480},{1,33,65..., dimensions={0}, use_global_device_ids=true | all-gather | bytes 2396160 | tf_op jit(solution)/shard_map/all_gather | solution.py:89
  84.3 0.1 fusion.62
  84.4 0.8 fusion.21
  85.2 1.6 %fusion.28 = f32[512,256]{1,0:T(8,128)} fusion(f32[512,256]{1,0:T(8,128)S(1)} %fusion.24, f32[512,256]{1,0:T(8,128)S(1)} %fusion.21, f32[8]{0:T(128)S(1)} %fusion.62, f16[8,520,256]{2,1,0:T(8,128)(2,1)S(1)} %bitcast.86, bf16[2,8,256,256]{3,2,1,0:T(8,128)(2,1)S(1)} %bitcast.81, s32[]{:T(128)S(6)} %select_n.14), kind=kOutput, calls=%fused_computation.26 | convolution fusion | flops 541327360 | bytes 4719108 | tf_op jit(solution)/shard_map/dot_general | solution.py:99
  (8 shorter events, 0.0 us)
Async XLA Ops:
  0.0 62.8 %copy-start = (bf16[4096,256]{1,0:T(8,128)(2,1)S(1)}, bf16[4096,256]{1,0:T(8,128)(2,1)}, u32[]{:S(2)}) copy-start(bf16[4096,256]{1,0:T(8,128)(2,1)} %param.4) | copy-start | bytes 6291460
  0.0 14.1 %copy-start.4 = (bf16[20,1,8,8,256]{4,3,2,1,0:T(8,128)(2,1)S(1)}, bf16[20,1,8,8,256]{4,3,2,1,0:T(8,128)(2,1)}, u32[]{:S(2)}) copy-start(bf16[20,1,8,8,256]{4,3,2,1,0:T(8,128)(2,1)} %param.3) | copy-start | bytes 1966084
  1.1 11.7 %copy-start.1 = (bf16[8,8,8,256]{3,2,1,0:T(8,128)(2,1)}, bf16[8,8,8,256]{3,2,1,0:T(8,128)(2,1)S(1)}, u32[]{:S(2)}) copy-start(bf16[8,8,8,256]{3,2,1,0:T(8,128)(2,1)S(1)} %slice_bitcast_fusion) | copy-start | bytes 786436
  2.0 13.6 %collective-permute-start = (bf16[8,6,8,256]{3,2,1,0:T(8,128)(2,1)}, bf16[8,6,8,256]{3,2,1,0:T(8,128)(2,1)}, u32[]{:S(2)}, u32[]{:S(2)}) collective-permute-start(bf16[8,6,8,256]{3,2,1,0:T(8,128)(2,1)} %get-tuple-element.13), channel_id=1, source_target_pairs={{0,4},{1,5},{2,6},{3,7},{4,8},{5,9},{6,10},{7,11},{8,12},{9,13},{1... | collective-permute-start | bytes 589832 | tf_op jit(solution)/shard_map/ppermute | solution.py:33
  5.5 10.0 %copy-start.5 = (f32[8,1,8,8]{3,2,1,0:T(8,128)S(1)}, f32[8,1,8,8]{3,2,1,0:T(8,128)}, u32[]{:S(2)}) copy-start(f32[8,1,8,8]{3,2,1,0:T(8,128)} %param.5) | copy-start | bytes 6148
  5.5 10.0 %collective-permute-start.1 = (bf16[8,6,8,256]{3,2,1,0:T(8,128)(2,1)}, bf16[8,6,8,256]{3,2,1,0:T(8,128)(2,1)}, u32[]{:S(2)}, u32[]{:S(2)}) collective-permute-start(bf16[8,6,8,256]{3,2,1,0:T(8,128)(2,1)} %get-tuple-element.14), channel_id=1, source_target_pairs={{4,0},{5,1},{6,2},{7,3},{8,4},{9,5},{10,6},{11,7},{12,8},{13,9},{1... | collective-permute-start | bytes 589832 | tf_op jit(solution)/shard_map/ppermute | solution.py:33
  8.9 8.0 %collective-permute-start.2 = (bf16[8,8,6,256]{3,2,1,0:T(8,128)(2,1)}, bf16[8,8,6,256]{3,2,1,0:T(8,128)(2,1)}, u32[]{:S(2)}, u32[]{:S(2)}) collective-permute-start(bf16[8,8,6,256]{3,2,1,0:T(8,128)(2,1)} %get-tuple-element.15), channel_id=1, source_target_pairs={{0,1},{1,2},{2,3},{4,5},{5,6},{6,7},{8,9},{9,10},{10,11},{12,13},{... | collective-permute-start | bytes 589832 | tf_op jit(solution)/shard_map/ppermute | solution.py:43
  12.8 7.9 %collective-permute-start.3 = (bf16[8,8,6,256]{3,2,1,0:T(8,128)(2,1)}, bf16[8,8,6,256]{3,2,1,0:T(8,128)(2,1)}, u32[]{:S(2)}, u32[]{:S(2)}) collective-permute-start(bf16[8,8,6,256]{3,2,1,0:T(8,128)(2,1)} %get-tuple-element.16), channel_id=1, source_target_pairs={{1,0},{2,1},{3,2},{5,4},{6,5},{7,6},{9,8},{10,9},{11,10},{13,12},{... | collective-permute-start | bytes 589832 | tf_op jit(solution)/shard_map/ppermute | solution.py:43
  15.5 5.2 %copy-start.2 = (bf16[8,8,8,256]{3,2,1,0:T(8,128)(2,1)S(1)}, bf16[8,8,8,256]{3,2,1,0:T(8,128)(2,1)}, u32[]{:S(2)}) copy-start(bf16[8,8,8,256]{3,2,1,0:T(8,128)(2,1)} %copy-done.1) | copy-start | bytes 786436
  15.5 6.6 %copy-start.3 = (f32[20,1,8,8,256]{4,3,2,1,0:T(8,128)S(1)}, f32[20,1,8,8,256]{4,3,2,1,0:T(8,128)}, u32[]{:S(2)}) copy-start(f32[20,1,8,8,256]{4,3,2,1,0:T(8,128)} %get-tuple-element.12) | copy-start | bytes 3932164
  28.3 38.0 %collective-permute-start.4 = (f16[520,256]{1,0:T(8,128)(2,1)S(1)}, f16[520,256]{1,0:T(8,128)(2,1)S(1)}, u32[]{:S(2)}, u32[]{:S(2)}) collective-permute-start(f16[520,256]{1,0:T(8,128)(2,1)S(1)} %concatenate.11), channel_id=1, source_target_pairs={{0,256},{32,288},{64,320},{96,352},{128,384},{160,416},{192,448},{... | collective-permute-start | bytes 798728 | tf_op jit(solution)/shard_map/ppermute | solution.py:120
